TPU v7x, 128 devices: a whole 4x4x4 slice. The times are simulated.
128 devices in a mesh: row: 8 (over y, z_hi), col: 16 (over x, z_lo, core).
Axes of the slice: x: 4, y: 4, z: 4 (z_hi: 2, z_lo: 2; z = z_hi * 2 + z_lo), core: 2. Of those that a mesh axis runs over, the one named last changes fastest.
Arguments:
- band_factors: bfloat16 [48, 48, 8, 256], P('col'), may hold values from -6 to 6
- pair_density: bfloat16 [48, 48, 16, 256], P('col'), may hold values from -6 to 6
- screened: bfloat16 [48, 48, 256, 256], P('col'), may hold values from -1 to 3, as said below
- coulomb: float32 [256], replicated, may hold values from 0.2 to 2
- window_mask: int32 [3, 48, 48], P(None, 'row'), may hold values 0 or 1
- trial_vector: bfloat16 [16, 48, 48], P(None, 'col'), may hold values from -0.0013809204 to 0.0013809204
Outputs:
- row_image: float32 [16, 3, 48], P('col', None, 'row')
- col_image: float32 [16, 48, 48], P(None, 'col', 'row')
Inputs may be any that keep to these rules, and one draw needn't show every extreme that they name: `screened`: every block is symmetric.
All inputs are finite; a program needn't handle non-finite values. No bound on the sum of `window_mask` on one device may be relied on, other than what follows from the above.
Results may differ from a plain program's by a relative error of at most 0.0041.
Values may be sent and summed in bfloat16 or wider, within the bound.
A program may use at most 192 MiB of HBM per device.

v0:
```python
import jax
import jax.numpy as jnp
from jax import lax
from jax.sharding import PartitionSpec as P

HIGHEST_PRECISION = lax.Precision.HIGHEST


def broadcast(block, axis, holder):
    block = jnp.where(lax.axis_index(axis) == holder, block, jnp.zeros_like(block))
    return lax.psum(block, axis)


def shifted(block, axis, distance):
    devices = range(lax.axis_size(axis))
    route = [(i - distance, i) for i in devices if i - distance in devices]
    return lax.ppermute(block, axis, route)


def slab_terms(
    row_bands,
    row_pairs,
    row_trial,
    row_lines,
    first_b,
    col_bands,
    col_pairs,
    col_trial,
    col_lines,
    blocks,
    q_values,
    kept_mask,
    coulomb,
):
    line_count, row_width = (row_bands.shape[0], row_bands.shape[1])
    mesh_side = col_bands.shape[1]
    band_half = row_bands.shape[2] // 2
    fourier = row_bands.shape[3]
    q_count = q_values.shape[0]
    within = jnp.arange(row_width, dtype=jnp.int32)
    places = (first_b + within[None, :] + q_values[:, None]) % mesh_side
    chosen_bands = jnp.take(col_bands, places, axis=1)
    chosen_pairs = jnp.take(col_pairs, places, axis=1)
    left_pair = (
        row_bands[:, None, :, :band_half, None, :] * chosen_bands[:, :, :, None, :band_half, :]
    )
    right_pair = (
        row_bands[:, None, :, band_half:, None, :] * chosen_bands[:, :, :, None, band_half:, :]
    )
    mixed_pair = jnp.einsum(
        "tqmg,qgh->tqmh",
        left_pair.reshape(line_count, q_count, row_width * band_half * band_half, fourier),
        blocks,
        preferred_element_type=jnp.float32,
    ).astype(jnp.bfloat16)
    mixed_pair = mixed_pair.reshape(line_count, q_count, row_width, band_half, band_half, fourier)
    direct = jnp.einsum(
        "tqiach,tqivwh->tqivawc", mixed_pair, right_pair, preferred_element_type=jnp.float32
    )
    direct = direct.reshape(
        line_count, q_count, row_width, band_half * band_half, band_half * band_half
    )
    scaled = (row_pairs.astype(jnp.float32) * coulomb).astype(jnp.bfloat16)
    exchange_term = jnp.einsum(
        "tisg,tqiug->tqisu", scaled, chosen_pairs, preferred_element_type=jnp.float32
    )
    kernel = 2.0 * exchange_term - direct
    row_place = row_lines[:, None] * mesh_side + first_b + within[None, :]
    col_place = col_lines[:, None, None] * mesh_side + places[None, :, :]
    kept = (col_place >= row_place[:, None, :]) & (kept_mask[:, None, :] > 0)
    kernel = jnp.where(kept[..., None, None], kernel, 0.0)
    chosen_trial = jnp.take(col_trial, places, axis=2)
    row_part = jnp.einsum("tqisu,utqi->sti", kernel, chosen_trial, precision=HIGHEST_PRECISION)
    strict = col_place > row_place[:, None, :]
    col_each = jnp.einsum(
        "tqisu,sti->utqi",
        jnp.where(strict[..., None, None], kernel, 0.0),
        row_trial,
        precision=HIGHEST_PRECISION,
    )
    onehot = (places[:, :, None] == jnp.arange(mesh_side, dtype=jnp.int32)[None, None, :]).astype(
        jnp.float32
    )
    col_part = jnp.einsum("utqi,qic->utc", col_each, onehot, precision=HIGHEST_PRECISION)
    return (row_part, col_part)


def add_into(total, part, start):
    piece = lax.dynamic_slice_in_dim(total, start, part.shape[1], 1)
    return lax.dynamic_update_slice_in_dim(total, piece + part, start, 1)


def local(band_factors, pair_density, screened, coulomb, window_mask, trial_vector):
    col_count = lax.axis_size("col")
    col_index = lax.axis_index("col")
    row_index = lax.axis_index("row")
    midway = col_count // 2
    band_lines, mesh_side = (band_factors.shape[0], band_factors.shape[1])
    row_width = window_mask.shape[1]
    first_b = row_index * row_width
    picked = (
        lax.dynamic_slice_in_dim(band_factors, first_b, row_width, 1),
        lax.dynamic_slice_in_dim(pair_density, first_b, row_width, 1),
        lax.dynamic_slice_in_dim(trial_vector, first_b, row_width, 2),
    )
    row_bands, row_pairs, row_trial = (
        broadcast(picked[0], "col", midway),
        broadcast(picked[1], "col", midway),
        broadcast(picked[2], "col", midway),
    )
    row_trial = row_trial.astype(jnp.float32)
    panel_first = band_lines * midway
    all_q = jnp.arange(mesh_side, dtype=jnp.int32)

    def compute_slab(
        row_start,
        col_start,
        line_count,
        col_band_first,
        col_bands,
        col_pairs,
        col_trial,
        blocks,
        q_values,
    ):
        row_lines = panel_first + row_start + jnp.arange(line_count, dtype=jnp.int32)
        col_lines = col_band_first + col_start + jnp.arange(line_count, dtype=jnp.int32)
        mask_rows = lax.dynamic_slice_in_dim(window_mask, row_start, line_count, 0)
        line_index = jnp.broadcast_to(
            (col_lines % mesh_side)[:, None, None], (line_count, row_width, 1)
        )
        kept_mask = jnp.take_along_axis(mask_rows, line_index, axis=2)[:, :, 0]
        return slab_terms(
            lax.dynamic_slice_in_dim(row_bands, row_start, line_count, 0),
            lax.dynamic_slice_in_dim(row_pairs, row_start, line_count, 0),
            lax.dynamic_slice_in_dim(row_trial, row_start, line_count, 1),
            row_lines,
            first_b,
            lax.dynamic_slice_in_dim(col_bands, col_start, line_count, 0),
            lax.dynamic_slice_in_dim(col_pairs, col_start, line_count, 0),
            lax.dynamic_slice_in_dim(col_trial, col_start, line_count, 1),
            col_lines,
            blocks,
            q_values,
            kept_mask,
            coulomb,
        )

    is_live = col_index >= midway
    live_flag = is_live.astype(jnp.int32)
    received = shifted((band_factors, pair_density, trial_vector), "col", -midway)
    col_bands = jnp.where(is_live, band_factors, received[0])
    col_pairs = jnp.where(is_live, pair_density, received[1])
    col_trial = jnp.where(is_live, trial_vector, received[2]).astype(jnp.float32)
    col_band_first = jnp.where(is_live, col_index, col_index + midway) * band_lines
    center = shifted(screened[0, mesh_side // 2 :], "col", midway)
    blocks = jnp.where(is_live, center, screened[0, : mesh_side // 2])
    q_values = all_q[: mesh_side // 2] + live_flag * (mesh_side // 2)
    row_part, col_part = compute_slab(
        0, 0, band_lines, col_band_first, col_bands, col_pairs, col_trial, blocks, q_values
    )
    row_total = row_part
    col_total = col_part
    below_rows = shifted(screened[1:], "col", midway + 1)
    for line_gap in range(1, band_lines):
        blocks = jnp.where(is_live, below_rows[band_lines - 1 - line_gap], screened[line_gap])
        row_start = live_flag * line_gap
        col_start = (1 - live_flag) * line_gap
        row_part, col_part = compute_slab(
            row_start,
            col_start,
            band_lines - line_gap,
            col_band_first,
            col_bands,
            col_pairs,
            col_trial,
            blocks,
            all_q,
        )
        row_total = add_into(row_total, row_part, row_start)
        col_total = add_into(col_total, col_part, col_start)
    returned = shifted(col_total, "col", midway)
    col_total = jnp.where(is_live, col_total + returned, 0.0)
    row_image = lax.psum_scatter(row_total, "col", scatter_dimension=0, tiled=True)
    col_image = lax.psum_scatter(col_total, "row", scatter_dimension=2, tiled=True)
    return (row_image, col_image)


def solution(mesh):
    placed = (
        P("col", None, None, None),
        P("col", None, None, None),
        P("col", None, None, None),
        P(),
        P(None, "row", None),
        P(None, "col", None),
    )
    return jax.shard_map(
        local,
        mesh=mesh,
        in_specs=placed,
        out_specs=(P("col", None, "row"), P(None, "col", "row")),
        check_vma=False,
    )
```

profile of v0, /device:TPU:0, one launch (start us, length us, event | category | flops | bytes accessed | tf_op | source)
XLA Modules:
  0.0 808.4 jit_solution(10363889306173101909)
XLA Ops:
  8.5 10.6 %slice.69 = bf16[2,48,256,256]{3,2,1,0:T(8,128)(2,1)} slice(bf16[3,48,256,256]{3,2,1,0:T(8,128)(2,1)} %param.8), slice={[1:3], [0:48], [0:256], [0:256]} | slice | bytes 25165824 | tf_op jit(solution)/shard_map/slice | solution.py:164
  19.1 9.2 %collective-permute-start.4 = (bf16[2,48,256,256]{3,2,1,0:T(8,128)(2,1)}, bf16[2,48,256,256]{3,2,1,0:T(8,128)(2,1)}, u32[]{:S(2)}, u32[]{:S(2)}) collective-permute-start(bf16[2,48,256,256]{3,2,1,0:T(8,128)(2,1)} %slice.69), channel_id=1, source_target_pairs={{0,9},{1,10},{2,11},{3,12},{4,13},{5,14},{6,15},{16,25},{17,26},{1... | collective-permute-start | bytes 37748744 | tf_op jit(solution)/shard_map/ppermute | solution.py:17
  34.8 8.9 %collective-permute-start.3 = (bf16[24,256,256]{2,1,0:T(8,128)(2,1)}, bf16[24,256,256]{2,1,0:T(8,128)(2,1)}, u32[]{:S(2)}, u32[]{:S(2)}) collective-permute-start(bf16[24,256,256]{2,1,0:T(8,128)(2,1)} %slice_bitcast_fusion), channel_id=1, source_target_pairs={{0,8},{1,9},{2,10},{3,11},{4,12},{5,13},{6,14},{7,15},{16,24},{17,... | collective-permute-start | bytes 9437192 | tf_op jit(solution)/shard_map/ppermute | solution.py:17
  49.7 332.8 %psum.23 = bf16[16,3,6]{0,2,1:T(8,128)(2,1)S(1)} all-reduce(bf16[16,3,6]{0,2,1:T(8,128)(2,1)S(1)} %broadcast_select_fusion.4), channel_id=1, replica_groups=mesh['row'=8,'col'=16] {'col'}, use_global_device_ids=true, to_apply=%region_3.4 | all-reduce | flops 288 | bytes 1152 | tf_op jit(solution)/shard_map/psum | solution.py:11
  396.3 35.1 %all-reduce.5.cloned.1.call-done = (bf16[3,6,8,256]{3,2,1,0:T(8,128)(2,1)}, bf16[3,6,16,256]{3,2,1,0:T(8,128)(2,1)}) async-done(((bf16[3,6,8,256]{3,2,1,0:T(8,128)(2,1)}, bf16[3,6,16,256]{3,2,1,0:T(8,128)(2,1)}), (bf16[3,6,8,256]{3,2,1,0:T(8,128)(2,1)}, bf16[3,6,16,256]{3,2,1,0:T(8,128)(2,1)})) %all-reduce.5.cloned.1.call-update) | async-done | bytes 221200 | tf_op jit(solution)/shard_map/psum | solution.py:11
  447.8 7.8 mul.255
  460.4 6.8 mul.239
  477.9 13.6 %gather_fusion.4 = bf16[288,2,16,256]{3,2,1,0:T(8,128)(2,1)} fusion(bf16[2,48,16,256]{3,2,1,0:T(8,128)(2,1)S(1)} %constant_dynamic-slice_fusion.8, s32[1024]{0:T(1024)S(1)} %pad_clamp_fusion), kind=kCustom, calls=%fused_computation.4 | custom fusion | bytes 9438336 | tf_op jit(solution)/shard_map/jit(_take)/gather | solution.py:43
  494.5 6.2 convert_bitcast_fusion.1
  500.7 5.7 reshape.941
  506.4 20.6 %convolution_bitcast_fusion.1 = f32[3,24,6,4,4,4,4]{6,5,4,3,2,1,0:T(4,128)} fusion(bf16[3,6,4,256]{3,2,1,0:T(4,128)(2,1)} %get-tuple-element.20, bf16[3,24,6,4,4,256]{5,4,3,2,0,1:T(4,128)(2,1)S(1)} %reshape.941, bf16[3,24,6,4,256]{4,3,0,2,1:T(4,128)(2,1)} %get-tuple-element.12), kind=kOutput, calls=%fused_computation.13 | convolution fusion | flops 63700992 | bytes 4902912 | tf_op jit(solution)/shard_map/tqiach,tqivwh->tqivawc/dot_general | solution.py:57
  526.9 13.2 %copy.66 = f32[3,24,6,4,4,4,4]{1,6,5,4,3,2,0:T(4,128)S(1)} copy(f32[3,24,6,4,4,4,4]{6,5,4,3,2,1,0:T(4,128)} %convolution_bitcast_fusion.1) | data formatting | bytes 884736 | tf_op jit(solution)/shard_map/tqiach,tqivwh->tqivawc/transpose | solution.py:57
  547.3 13.7 %fusion.23 = f32[3,6,1,24,16]{4,2,3,1,0:T(1,128)} fusion(f32[3,24,6,16,16]{3,4,1,2,0:T(8,128)S(1)} %fusion.20, pred[3,24,6]{1,2,0:T(8,128)(4,1)S(1)} %copy-done.23, bf16[16,3,6,1,1]{0,2,1,3,4:T(8,128)(2,1)S(1)} %bitcast.283), kind=kOutput, calls=%fused_computation.45 | convolution fusion | flops 1437696 | bytes 471024 | tf_op jit(solution)/shard_map/tqisu,sti->utqi/dot_general | solution.py:75
  567.0 9.1 %convert_bitcast_fusion = bf16[2,48,96,256]{3,2,0,1:T(8,128)(2,1)} fusion(bf16[2,48,96,256]{3,2,0,1:T(8,128)(2,1)} %mul.255, bf16[2,48,256,256]{3,2,1,0:T(8,128)(2,1)} %collective-permute-done.4, bf16[3,48,256,256]{3,2,1,0:T(8,128)(2,1)} %param.8, pred[]{:T(512)S(6)} %ge.124, bf16[2,96,256]{2,1,0:T(8,128)(2,1)S(1)} %copy-done.13), kind=kOutput, calls=%fused_computation.34 | convolution fusion | flops 1222901760 | bytes 22118400 | tf_op jit(solution)/shard_map/tqmg,qgh->tqmh/dot_general | solution.py:50
  576.1 7.8 reshape.943
  583.9 46.0 %convolution_bitcast_fusion = f32[2,48,6,4,4,4,4]{6,5,4,3,2,1,0:T(4,128)} fusion(bf16[2,6,4,256]{3,2,1,0:T(4,128)(2,1)S(1)} %copy-done.21, bf16[2,48,6,4,4,256]{5,4,3,2,0,1:T(4,128)(2,1)} %reshape.943, bf16[2,48,6,4,256]{4,3,0,2,1:T(4,128)(2,1)S(1)} %copy-done.5), kind=kOutput, calls=%fused_computation.12 | convolution fusion | flops 84934656 | bytes 6512640 | tf_op jit(solution)/shard_map/tqiach,tqivwh->tqivawc/dot_general | solution.py:57
  629.8 15.6 %copy.75 = f32[2,48,6,4,4,4,4]{1,6,5,4,3,2,0:T(4,128)S(1)} copy(f32[2,48,6,4,4,4,4]{6,5,4,3,2,1,0:T(4,128)} %convolution_bitcast_fusion) | data formatting | bytes 1179648 | tf_op jit(solution)/shard_map/tqiach,tqivwh->tqivawc/transpose | solution.py:57
  649.0 5.9 multiply_reduce_fusion.1
  657.4 8.2 %convert_bitcast_fusion.2 = bf16[1,48,96,256]{3,2,1,0:T(8,128)(2,1)} fusion(bf16[2,48,256,256]{3,2,1,0:T(8,128)(2,1)} %collective-permute-done.4, bf16[3,48,256,256]{3,2,1,0:T(8,128)(2,1)} %param.8, pred[]{:T(512)S(6)} %ge.124, bf16[48,96,256]{2,1,0:T(8,128)(2,1)S(1)} %copy-done.4, bf16[96,256]{1,0:T(8,128)(2,1)S(1)} %copy-done.16), kind=kOutput, calls=%fused_computation.69 | convolution fusion | flops 613023744 | bytes 17350656 | tf_op jit(solution)/shard_map/tqmg,qgh->tqmh/dot_general | solution.py:50
  669.8 12.8 %convolution_bitcast_fusion.2 = f32[1,48,6,4,4,4,4]{6,5,4,3,2,1,0:T(4,128)} fusion(bf16[48,6,4,4,256,1]{4,3,2,1,0,5:T(4,128)(2,1)S(1)} %reshape.1099, bf16[48,6,4,256]{3,2,1,0:T(4,128)(2,1)S(1)} %copy-done.8, bf16[6,4,256]{2,1,0:T(4,128)(2,1)S(1)} %copy-done.24), kind=kOutput, calls=%fused_computation.24 | convolution fusion | flops 42467328 | bytes 3256320 | tf_op jit(solution)/shard_map/tqiach,tqivwh->tqivawc/dot_general | solution.py:57
  682.6 8.2 %copy.82 = f32[1,48,6,4,4,4,4]{1,6,5,4,3,2,0:T(4,128)S(1)} copy(f32[1,48,6,4,4,4,4]{6,5,4,3,2,1,0:T(4,128)} %convolution_bitcast_fusion.2) | data formatting | bytes 589824 | tf_op jit(solution)/shard_map/tqiach,tqivwh->tqivawc/transpose | solution.py:57
  693.2 4.4 fusion.43
  700.9 55.7 %all-reduce = f32[16,3,6]{2,1,0:T(4,128)S(1)} all-reduce(f32[16,3,6]{2,1,0:T(4,128)S(1)} %copy.84), channel_id=2, replica_groups=mesh['row'=8,'col'=16] {'col'}, use_global_device_ids=true, to_apply=%region_2.3.clone | all-reduce | flops 288 | bytes 2304
  757.9 42.8 %all-reduce.1 = f32[16,3,48]{0,1,2:T(4,128)S(1)} all-reduce(f32[16,3,48]{0,1,2:T(4,128)S(1)} %copy.87), channel_id=3, replica_groups=mesh['row'=8,'col'=16] {'row'}, use_global_device_ids=true, to_apply=%region_4.5.clone | all-reduce | flops 2304 | bytes 18432
  (220 shorter events, 92.1 us)
Async XLA Ops:
  7.2 39.3 %copy-start = (s32[3,6,48]{2,1,0:T(8,128)S(1)}, s32[3,6,48]{2,1,0:T(8,128)}, u32[]{:S(2)}) copy-start(s32[3,6,48]{2,1,0:T(8,128)} %param.10) | copy-start | bytes 10372
  7.2 21.1 %copy-start.17 = (bf16[16,3,48]{2,0,1:T(8,128)(2,1)S(1)}, bf16[16,3,48]{2,0,1:T(8,128)(2,1)}, u32[]{:S(2)}) copy-start(bf16[16,3,48]{2,0,1:T(8,128)(2,1)} %param.11) | copy-start | bytes 13828
  7.2 424.3 %all-reduce.5.cloned.1.call-start = ((), (), s32[]{:S(2)}) async-start(), calls=%async_computation | async-start | bytes 442368 | tf_op jit(solution)/shard_map/psum | solution.py:11
  7.2 430.2 %collective-permute-start.2 = (bf16[3,48,8,256]{3,2,1,0:T(8,128)(2,1)}, bf16[3,48,8,256]{3,2,1,0:T(8,128)(2,1)S(1)}, u32[]{:S(2)}, u32[]{:S(2)}) collective-permute-start(bf16[3,48,8,256]{3,2,1,0:T(8,128)(2,1)} %param.6), channel_id=1, source_target_pairs={{8,0},{9,1},{10,2},{11,3},{12,4},{13,5},{14,6},{15,7},{24,16},{25,... | collective-permute-start | bytes 1769480 | tf_op jit(solution)/shard_map/ppermute | solution.py:17
  19.1 26.2 %copy-start.6 = (bf16[3,48,8,256]{3,2,1,0:T(8,128)(2,1)S(1)}, bf16[3,48,8,256]{3,2,1,0:T(8,128)(2,1)}, u32[]{:S(2)}) copy-start(bf16[3,48,8,256]{3,2,1,0:T(8,128)(2,1)} %param.6) | copy-start | bytes 1769476
  19.1 547.9 %collective-permute-start.4 = (bf16[2,48,256,256]{3,2,1,0:T(8,128)(2,1)}, bf16[2,48,256,256]{3,2,1,0:T(8,128)(2,1)}, u32[]{:S(2)}, u32[]{:S(2)}) collective-permute-start(bf16[2,48,256,256]{3,2,1,0:T(8,128)(2,1)} %slice.69), channel_id=1, source_target_pairs={{0,9},{1,10},{2,11},{3,12},{4,13},{5,14},{6,15},{16,25},{17,26},{1... | collective-permute-start | bytes 37748744 | tf_op jit(solution)/shard_map/ppermute | solution.py:17
  28.3 360.6 %collective-permute-start = (bf16[16,3,48]{2,0,1:T(8,128)(2,1)S(1)}, bf16[16,3,48]{2,0,1:T(8,128)(2,1)S(1)}, u32[]{:S(2)}, u32[]{:S(2)}) collective-permute-start(bf16[16,3,48]{2,0,1:T(8,128)(2,1)S(1)} %copy-done.17), channel_id=1, source_target_pairs={{8,0},{9,1},{10,2},{11,3},{12,4},{13,5},{14,6},{15,7},{24,16},{25,... | collective-permute-start | bytes 13832 | tf_op jit(solution)/shard_map/ppermute | solution.py:17
  29.6 444.0 %collective-permute-start.1 = (bf16[3,48,16,256]{3,2,1,0:T(8,128)(2,1)}, bf16[3,48,16,256]{3,2,1,0:T(8,128)(2,1)}, u32[]{:S(2)}, u32[]{:S(2)}) collective-permute-start(bf16[3,48,16,256]{3,2,1,0:T(8,128)(2,1)} %param.7), channel_id=1, source_target_pairs={{8,0},{9,1},{10,2},{11,3},{12,4},{13,5},{14,6},{15,7},{24,16},{25,... | collective-permute-start | bytes 3538952 | tf_op jit(solution)/shard_map/ppermute | solution.py:17
  34.8 352.2 %copy-start.35 = (u32[128]{0:T(128)S(1)}, u32[128]{0:T(128)}, u32[]{:S(2)}) copy-start(u32[128]{0:T(128)} %constant.311) | copy-start | bytes 1540
  34.8 352.8 %copy-start.34 = (u32[128]{0:T(128)S(1)}, u32[128]{0:T(128)}, u32[]{:S(2)}) copy-start(u32[128]{0:T(128)} %constant.307) | copy-start | bytes 1540
  34.8 459.6 %collective-permute-start.3 = (bf16[24,256,256]{2,1,0:T(8,128)(2,1)}, bf16[24,256,256]{2,1,0:T(8,128)(2,1)}, u32[]{:S(2)}, u32[]{:S(2)}) collective-permute-start(bf16[24,256,256]{2,1,0:T(8,128)(2,1)} %slice_bitcast_fusion), channel_id=1, source_target_pairs={{0,8},{1,9},{2,10},{3,11},{4,12},{5,13},{6,14},{7,15},{16,24},{17,... | collective-permute-start | bytes 9437192 | tf_op jit(solution)/shard_map/ppermute | solution.py:17
  49.0 344.9 %copy-start.18 = (s32[24,6]{0,1:T(8,128)}, s32[24,6]{0,1:T(8,128)S(1)}, u32[]{:S(2)}) copy-start(s32[24,6]{0,1:T(8,128)S(1)} %copy.60) | copy-start | bytes 1732
  384.9 9.0 %copy-start.27 = (pred[48,6]{0,1:T(8,128)(4,1)}, pred[48,6]{0,1:T(8,128)(4,1)S(1)}, u32[]{:S(2)}) copy-start(pred[48,6]{0,1:T(8,128)(4,1)S(1)} %get-tuple-element.30) | copy-start | bytes 868
  386.4 82.7 %copy-start.10 = (pred[48,6]{1,0:T(8,128)(4,1)}, pred[48,6]{1,0:T(8,128)(4,1)S(1)}, u32[]{:S(2)}) copy-start(pred[48,6]{1,0:T(8,128)(4,1)S(1)} %copy.68) | copy-start | bytes 868
  447.8 7.8 copy-start.2
  547.3 19.4 %copy-start.19 = (s32[24,6]{0,1:T(8,128)S(1)}, s32[24,6]{0,1:T(8,128)}, u32[]{:S(2)}) copy-start(s32[24,6]{0,1:T(8,128)} %copy-done.18) | copy-start | bytes 1732
  576.1 7.8 copy-start.5
  576.1 7.8 copy-start.21
  682.6 10.6 %copy-start.3 = (bf16[288,16,256]{2,1,0:T(8,128)(2,1)S(1)}, bf16[288,16,256]{2,1,0:T(8,128)(2,1)}, u32[]{:S(2)}) copy-start(bf16[288,16,256]{2,1,0:T(8,128)(2,1)} %gather_fusion.7) | copy-start | bytes 7077892
  682.6 10.6 %copy-start.11 = (pred[48,6]{1,0:T(8,128)(4,1)S(1)}, pred[48,6]{1,0:T(8,128)(4,1)}, u32[]{:S(2)}) copy-start(pred[48,6]{1,0:T(8,128)(4,1)} %copy-done.10) | copy-start | bytes 868
  682.6 10.6 %copy-start.12 = (f32[6,48,16]{2,1,0:T(8,128)S(1)}, f32[6,48,16]{2,1,0:T(8,128)}, u32[]{:S(2)}) copy-start(f32[6,48,16]{2,1,0:T(8,128)} %copy.144) | copy-start | bytes 55300
  682.6 10.6 %copy-start.31 = (pred[48,6]{0,1:T(8,128)(4,1)S(1)}, pred[48,6]{0,1:T(8,128)(4,1)}, u32[]{:S(2)}) copy-start(pred[48,6]{0,1:T(8,128)(4,1)} %get-tuple-element.29) | copy-start | bytes 868
  693.2 108.2 %copy-start.1 = (s32[3,6,48]{2,1,0:T(8,128)S(1)}, s32[3,6,48]{2,1,0:T(8,128)}, u32[]{:S(2)}) copy-start(s32[3,6,48]{2,1,0:T(8,128)} %param.10) | copy-start | bytes 10372
  699.4 58.4 %collective-permute-start.5 = (f32[16,3,48]{2,0,1:T(8,128)S(1)}, f32[16,3,48]{2,0,1:T(8,128)S(1)}, u32[]{:S(2)}, u32[]{:S(2)}) collective-permute-start(f32[16,3,48]{2,0,1:T(8,128)S(1)} %fusion.75), channel_id=1, source_target_pairs={{0,8},{1,9},{2,10},{3,11},{4,12},{5,13},{6,14},{7,15},{16,24},{17,... | collective-permute-start | bytes 27656 | tf_op jit(solution)/shard_map/ppermute | solution.py:17
  (19 other events, 73.9 us)
Sparse Core Ops, SparseCore 0:
  46.1 385.3 all-reduce.4
where the time goes:
time: 813 us; the launch traced here: 808 us
  blocking collectives  431 us (53%)
  local copies, waits for them, and re-layouts  153 us (19%)
  matrix products  136 us (17%)
  waiting for transfers between devices  35.2 us (4%)
  starting transfers between devices  23.3 us (3%)
  between operations  15.8 us (2%)
  other arithmetic  14 us (2%)
    psum x1, blocking collectives, broadcast(): return lax.psum(block, axis)  333 us
    unnamed x2, blocking collectives  98.5 us
    dot_general x3, matrix products, slab_terms(): jnp.einsum('tqiach,tqivwh->tqivawc', mixed_pair, right_pair, preferred_el...  79.3 us
    transpose x3, local copies, waits for them, and re-layouts, slab_terms(): jnp.einsum('tqiach,tqivwh->tqivawc', mixed_pair, right_pair, preferred_el...  37 us
    psum x1, waiting for transfers between devices, broadcast(): return lax.psum(block, axis)  35.1 us
    mul x12, local copies, waits for them, and re-layouts, slab_terms(): row_bands[:, None, :, :band_half, None, :]  24.9 us
    dot_general x3, matrix products, slab_terms(): jnp.einsum('tqmg,qgh->tqmh', left_pair.reshape(line_count, q_count, row_w...  23.5 us
    ppermute x6, starting transfers between devices, shifted(): return lax.ppermute(block, axis, route)  23.2 us
  transfers between devices with their start and end apart: 7, of which 1 were waited for; matrix products, arithmetic and copies ran while one was open for 21% of the time, Pallas kernels for 0%

commit v1 on v0

--- a/solution.py
+++ b/solution.py
@@ -8,7 +8,7 @@
 
 def broadcast(block, axis, holder):
     block = jnp.where(lax.axis_index(axis) == holder, block, jnp.zeros_like(block))
-    return lax.psum(block, axis)
+    return lax.all_gather(block, axis).sum(axis=0)
 
 
 def shifted(block, axis, distance):

time: 813 us -> 767 us (0.943)
  waiting for transfers between devices: 35.2 us -> 0.05 us
  matrix products: 136 us -> 124 us
    psum x1 -> x0, blocking collectives: 333 us -> none  [broadcast(): return lax.psum(block, axis)]
    all_gather x0 -> x1, blocking collectives: none -> 333 us  [broadcast(): return lax.all_gather(block, axis).sum(axis=0)]
    psum x1 -> x0, waiting for transfers between devices: 35.1 us -> none  [broadcast(): return lax.psum(block, axis)]
    dot_general x1 -> x0, matrix products: 13.7 us -> none  [slab_terms(): jnp.einsum('tqisu,sti->utqi', jnp.where(strict[..., None, None], kernel,...]
  transfers between devices with their start and end apart: 7 -> 8, of which waited for: 1 -> 0; matrix products, arithmetic and copies ran while one was open for 21% -> 21% of each run, Pallas kernels for 0% -> 0%
where the time goes in v1:
time: 767 us; the launch traced here: 762 us
  blocking collectives  430 us (56%)
  local copies, waits for them, and re-layouts  151 us (20%)
  matrix products  124 us (16%)
  starting transfers between devices  23.2 us (3%)
  other arithmetic  18.4 us (2%)
  between operations  15.8 us (2%)
    all_gather x1, blocking collectives, broadcast(): return lax.all_gather(block, axis).sum(axis=0)  333 us
    unnamed x2, blocking collectives  96.9 us
    dot_general x3, matrix products, slab_terms(): jnp.einsum('tqiach,tqivwh->tqivawc', mixed_pair, right_pair, preferred_el...  79.3 us
    transpose x3, local copies, waits for them, and re-layouts, slab_terms(): jnp.einsum('tqiach,tqivwh->tqivawc', mixed_pair, right_pair, preferred_el...  37 us
    mul x12, local copies, waits for them, and re-layouts, slab_terms(): row_bands[:, None, :, :band_half, None, :]  24.7 us
    dot_general x3, matrix products, slab_terms(): jnp.einsum('tqmg,qgh->tqmh', left_pair.reshape(line_count, q_count, row_w...  23.9 us
    ppermute x6, starting transfers between devices, shifted(): return lax.ppermute(block, axis, route)  23.1 us
    gather x3, local copies, waits for them, and re-layouts, slab_terms(): chosen_pairs = jnp.take(col_pairs, places, axis=1)  19.4 us
  transfers between devices with their start and end apart: 8, of which 0 were waited for; matrix products, arithmetic and copies ran while one was open for 21% of the time, Pallas kernels for 0%

profile of v1, /device:TPU:0, one launch (start us, length us, event | category | flops | bytes accessed | tf_op | source)
XLA Modules:
  0.0 762.1 jit_solution(2657715709119834051)
XLA Ops:
  10.2 10.6 %slice.69 = bf16[2,48,256,256]{3,2,1,0:T(8,128)(2,1)} slice(bf16[3,48,256,256]{3,2,1,0:T(8,128)(2,1)} %param.8), slice={[1:3], [0:48], [0:256], [0:256]} | slice | bytes 25165824 | tf_op jit(solution)/shard_map/slice | solution.py:164
  20.7 9.1 %collective-permute-start.4 = (bf16[2,48,256,256]{3,2,1,0:T(8,128)(2,1)}, bf16[2,48,256,256]{3,2,1,0:T(8,128)(2,1)}, u32[]{:S(2)}, u32[]{:S(2)}) collective-permute-start(bf16[2,48,256,256]{3,2,1,0:T(8,128)(2,1)} %slice.69), channel_id=1, source_target_pairs={{0,9},{1,10},{2,11},{3,12},{4,13},{5,14},{6,15},{16,25},{17,26},{1... | collective-permute-start | bytes 37748744 | tf_op jit(solution)/shard_map/ppermute | solution.py:17
  36.4 8.9 %collective-permute-start.3 = (bf16[24,256,256]{2,1,0:T(8,128)(2,1)}, bf16[24,256,256]{2,1,0:T(8,128)(2,1)}, u32[]{:S(2)}, u32[]{:S(2)}) collective-permute-start(bf16[24,256,256]{2,1,0:T(8,128)(2,1)} %slice_bitcast_fusion), channel_id=1, source_target_pairs={{0,8},{1,9},{2,10},{3,11},{4,12},{5,13},{6,14},{7,15},{16,24},{17,... | collective-permute-start | bytes 9437192 | tf_op jit(solution)/shard_map/ppermute | solution.py:17
  50.4 332.7 %all-gather.2 = bf16[256,3,6]{2,0,1:T(8,128)(2,1)S(1)} all-gather(bf16[16,3,6]{2,0,1:T(8,128)(2,1)S(1)} %dynamic-slice_select_fusion.2), channel_id=4, replica_groups=mesh['row'=8,'col'=16] {'col'}, dimensions={0}, use_global_device_ids=true | all-gather | bytes 9792 | tf_op jit(solution)/shard_map/all_gather | solution.py:11
  407.4 7.7 %mul.255 = bf16[2,48,96,256]{3,2,0,1:T(8,128)(2,1)} reshape(bf16[2,48,6,4,4,256]{5,4,3,2,0,1:T(4,128)(2,1)} %mul.254) | data formatting | bytes 9437184 | tf_op jit(solution)/shard_map/mul | solution.py:45
  419.8 6.8 mul.239
  437.3 13.5 %gather_fusion.4 = bf16[288,2,16,256]{3,2,1,0:T(8,128)(2,1)} fusion(bf16[2,48,16,256]{3,2,1,0:T(8,128)(2,1)S(1)} %constant_dynamic-slice_fusion.6, s32[1024]{0:T(1024)S(1)} %pad_clamp_fusion), kind=kCustom, calls=%fused_computation.4 | custom fusion | bytes 9438336 | tf_op jit(solution)/shard_map/jit(_take)/gather | solution.py:43
  458.6 6.2 convert_bitcast_fusion.1
  464.8 5.7 reshape.941
  470.5 20.4 %convolution_bitcast_fusion.1 = f32[3,24,6,4,4,4,4]{6,5,4,3,2,1,0:T(4,128)} fusion(bf16[3,6,4,256]{3,2,1,0:T(4,128)(2,1)} %get-tuple-element.18, bf16[3,24,6,4,4,256]{5,4,3,2,0,1:T(4,128)(2,1)S(1)} %reshape.941, bf16[3,24,6,4,256]{4,3,0,2,1:T(4,128)(2,1)} %get-tuple-element.10), kind=kOutput, calls=%fused_computation.13 | convolution fusion | flops 63700992 | bytes 4902912 | tf_op jit(solution)/shard_map/tqiach,tqivwh->tqivawc/dot_general | solution.py:57
  490.8 13.2 %copy.64 = f32[3,24,6,4,4,4,4]{1,6,5,4,3,2,0:T(4,128)S(1)} copy(f32[3,24,6,4,4,4,4]{6,5,4,3,2,1,0:T(4,128)} %convolution_bitcast_fusion.1) | data formatting | bytes 884736 | tf_op jit(solution)/shard_map/tqiach,tqivwh->tqivawc/transpose | solution.py:57
  509.9 5.8 multiply_reduce_fusion.2
  521.8 9.5 %convert_bitcast_fusion = bf16[2,48,96,256]{3,2,0,1:T(8,128)(2,1)} fusion(bf16[2,48,96,256]{3,2,0,1:T(8,128)(2,1)} %mul.255, bf16[2,48,256,256]{3,2,1,0:T(8,128)(2,1)} %collective-permute-done.4, bf16[3,48,256,256]{3,2,1,0:T(8,128)(2,1)} %param.8, pred[]{:T(512)S(6)} %ge.124, bf16[2,96,256]{2,1,0:T(8,128)(2,1)S(1)} %copy-done.14), kind=kOutput, calls=%fused_computation.34 | convolution fusion | flops 1222901760 | bytes 22118400 | tf_op jit(solution)/shard_map/tqmg,qgh->tqmh/dot_general | solution.py:50
  531.2 7.8 %reshape.943 = bf16[2,48,6,4,4,256]{5,4,3,2,0,1:T(4,128)(2,1)} reshape(bf16[2,48,96,256]{3,2,0,1:T(8,128)(2,1)} %convert_bitcast_fusion) | data formatting | bytes 9437184 | tf_op jit(solution)/shard_map/reshape | solution.py:56
  539.1 46.0 %convolution_bitcast_fusion = f32[2,48,6,4,4,4,4]{6,5,4,3,2,1,0:T(4,128)} fusion(bf16[2,6,4,256]{3,2,1,0:T(4,128)(2,1)S(1)} %copy-done.20, bf16[2,48,6,4,4,256]{5,4,3,2,0,1:T(4,128)(2,1)} %reshape.943, bf16[2,48,6,4,256]{4,3,0,2,1:T(4,128)(2,1)S(1)} %copy-done.4), kind=kOutput, calls=%fused_computation.12 | convolution fusion | flops 84934656 | bytes 6512640 | tf_op jit(solution)/shard_map/tqiach,tqivwh->tqivawc/dot_general | solution.py:57
  585.0 15.6 %copy.73 = f32[2,48,6,4,4,4,4]{1,6,5,4,3,2,0:T(4,128)S(1)} copy(f32[2,48,6,4,4,4,4]{6,5,4,3,2,1,0:T(4,128)} %convolution_bitcast_fusion) | data formatting | bytes 1179648 | tf_op jit(solution)/shard_map/tqiach,tqivwh->tqivawc/transpose | solution.py:57
  604.2 5.9 multiply_reduce_fusion.1
  612.4 8.2 %convert_bitcast_fusion.2 = bf16[1,48,96,256]{3,2,1,0:T(8,128)(2,1)} fusion(bf16[2,48,256,256]{3,2,1,0:T(8,128)(2,1)} %collective-permute-done.4, bf16[3,48,256,256]{3,2,1,0:T(8,128)(2,1)} %param.8, pred[]{:T(512)S(6)} %ge.124, bf16[48,96,256]{2,1,0:T(8,128)(2,1)S(1)} %copy-done.3, bf16[96,256]{1,0:T(8,128)(2,1)S(1)} %copy-done.15), kind=kOutput, calls=%fused_computation.68 | convolution fusion | flops 613023744 | bytes 17350656 | tf_op jit(solution)/shard_map/tqmg,qgh->tqmh/dot_general | solution.py:50
  620.7 4.1 reshape.1102
  624.8 13.0 %convolution_bitcast_fusion.2 = f32[1,48,6,4,4,4,4]{6,5,4,3,2,1,0:T(4,128)} fusion(bf16[48,6,4,4,256,1]{4,3,2,1,0,5:T(4,128)(2,1)S(1)} %reshape.1102, bf16[48,6,4,256]{3,2,1,0:T(4,128)(2,1)S(1)} %copy-done.7, bf16[6,4,256]{2,1,0:T(4,128)(2,1)S(1)} %copy-done.23), kind=kOutput, calls=%fused_computation.24 | convolution fusion | flops 42467328 | bytes 3256320 | tf_op jit(solution)/shard_map/tqiach,tqivwh->tqivawc/dot_general | solution.py:57
  637.8 8.2 %copy.80 = f32[1,48,6,4,4,4,4]{1,6,5,4,3,2,0:T(4,128)S(1)} copy(f32[1,48,6,4,4,4,4]{6,5,4,3,2,1,0:T(4,128)} %convolution_bitcast_fusion.2) | data formatting | bytes 589824 | tf_op jit(solution)/shard_map/tqiach,tqivwh->tqivawc/transpose | solution.py:57
  648.5 4.5 fusion.41
  656.2 53.0 %all-reduce = f32[16,3,6]{2,1,0:T(4,128)S(1)} all-reduce(f32[16,3,6]{2,1,0:T(4,128)S(1)} %copy.82), channel_id=5, replica_groups=mesh['row'=8,'col'=16] {'col'}, use_global_device_ids=true, to_apply=%region_2.3.clone | all-reduce | flops 288 | bytes 2304
  710.6 43.9 %all-reduce.1 = f32[16,3,48]{0,1,2:T(4,128)S(1)} all-reduce(f32[16,3,48]{0,1,2:T(4,128)S(1)} %copy.85), channel_id=6, replica_groups=mesh['row'=8,'col'=16] {'row'}, use_global_device_ids=true, to_apply=%region_4.5.clone | all-reduce | flops 2304 | bytes 18432
  (222 shorter events, 86.2 us)
Async XLA Ops:
  7.2 40.1 %copy-start = (s32[3,6,48]{2,1,0:T(8,128)S(1)}, s32[3,6,48]{2,1,0:T(8,128)}, u32[]{:S(2)}) copy-start(s32[3,6,48]{2,1,0:T(8,128)} %param.10) | copy-start | bytes 10372
  7.2 446.6 %all-gather.8.cloned.1.call-start = ((), (), s32[]{:S(2)}) async-start(), calls=%async_computation.1 | async-start | bytes 1253376 | tf_op jit(solution)/shard_map/all_gather | solution.py:11
  8.8 21.0 %copy-start.16 = (bf16[16,3,48]{2,0,1:T(8,128)(2,1)S(1)}, bf16[16,3,48]{2,0,1:T(8,128)(2,1)}, u32[]{:S(2)}) copy-start(bf16[16,3,48]{2,0,1:T(8,128)(2,1)} %param.11) | copy-start | bytes 13828
  8.8 498.4 %all-gather.6.cloned.1.call-start = ((), (), s32[]{:S(2)}) async-start(), calls=%async_computation | async-start | bytes 2506752 | tf_op jit(solution)/shard_map/all_gather | solution.py:11
  8.9 389.5 %collective-permute-start.2 = (bf16[3,48,8,256]{3,2,1,0:T(8,128)(2,1)}, bf16[3,48,8,256]{3,2,1,0:T(8,128)(2,1)S(1)}, u32[]{:S(2)}, u32[]{:S(2)}) collective-permute-start(bf16[3,48,8,256]{3,2,1,0:T(8,128)(2,1)} %param.6), channel_id=1, source_target_pairs={{8,0},{9,1},{10,2},{11,3},{12,4},{13,5},{14,6},{15,7},{24,16},{25,... | collective-permute-start | bytes 1769480 | tf_op jit(solution)/shard_map/ppermute | solution.py:17
  20.7 501.0 %collective-permute-start.4 = (bf16[2,48,256,256]{3,2,1,0:T(8,128)(2,1)}, bf16[2,48,256,256]{3,2,1,0:T(8,128)(2,1)}, u32[]{:S(2)}, u32[]{:S(2)}) collective-permute-start(bf16[2,48,256,256]{3,2,1,0:T(8,128)(2,1)} %slice.69), channel_id=1, source_target_pairs={{0,9},{1,10},{2,11},{3,12},{4,13},{5,14},{6,15},{16,25},{17,26},{1... | collective-permute-start | bytes 37748744 | tf_op jit(solution)/shard_map/ppermute | solution.py:17
  29.8 360.7 %collective-permute-start = (bf16[16,3,48]{2,0,1:T(8,128)(2,1)S(1)}, bf16[16,3,48]{2,0,1:T(8,128)(2,1)S(1)}, u32[]{:S(2)}, u32[]{:S(2)}) collective-permute-start(bf16[16,3,48]{2,0,1:T(8,128)(2,1)S(1)} %copy-done.16), channel_id=1, source_target_pairs={{8,0},{9,1},{10,2},{11,3},{12,4},{13,5},{14,6},{15,7},{24,16},{25,... | collective-permute-start | bytes 13832 | tf_op jit(solution)/shard_map/ppermute | solution.py:17
  31.1 401.9 %collective-permute-start.1 = (bf16[3,48,16,256]{3,2,1,0:T(8,128)(2,1)}, bf16[3,48,16,256]{3,2,1,0:T(8,128)(2,1)}, u32[]{:S(2)}, u32[]{:S(2)}) collective-permute-start(bf16[3,48,16,256]{3,2,1,0:T(8,128)(2,1)} %param.7), channel_id=1, source_target_pairs={{8,0},{9,1},{10,2},{11,3},{12,4},{13,5},{14,6},{15,7},{24,16},{25,... | collective-permute-start | bytes 3538952 | tf_op jit(solution)/shard_map/ppermute | solution.py:17
  36.4 352.2 %copy-start.32 = (u32[128]{0:T(128)S(1)}, u32[128]{0:T(128)}, u32[]{:S(2)}) copy-start(u32[128]{0:T(128)} %constant.315) | copy-start | bytes 1540
  36.4 352.9 %copy-start.31 = (u32[128]{0:T(128)S(1)}, u32[128]{0:T(128)}, u32[]{:S(2)}) copy-start(u32[128]{0:T(128)} %constant.311) | copy-start | bytes 1540
  36.4 422.2 %collective-permute-start.3 = (bf16[24,256,256]{2,1,0:T(8,128)(2,1)}, bf16[24,256,256]{2,1,0:T(8,128)(2,1)}, u32[]{:S(2)}, u32[]{:S(2)}) collective-permute-start(bf16[24,256,256]{2,1,0:T(8,128)(2,1)} %slice_bitcast_fusion), channel_id=1, source_target_pairs={{0,8},{1,9},{2,10},{3,11},{4,12},{5,13},{6,14},{7,15},{16,24},{17,... | collective-permute-start | bytes 9437192 | tf_op jit(solution)/shard_map/ppermute | solution.py:17
  49.6 340.9 %copy-start.17 = (s32[24,6]{0,1:T(8,128)}, s32[24,6]{0,1:T(8,128)S(1)}, u32[]{:S(2)}) copy-start(s32[24,6]{0,1:T(8,128)S(1)} %copy.58) | copy-start | bytes 1732
  384.4 6.2 copy-start.26
  385.9 14.5 %copy-start.9 = (pred[48,6]{1,0:T(8,128)(4,1)}, pred[48,6]{1,0:T(8,128)(4,1)S(1)}, u32[]{:S(2)}) copy-start(pred[48,6]{1,0:T(8,128)(4,1)S(1)} %copy.66) | copy-start | bytes 868
  419.8 8.6 %copy-start.10 = (pred[48,6]{1,0:T(8,128)(4,1)S(1)}, pred[48,6]{1,0:T(8,128)(4,1)}, u32[]{:S(2)}) copy-start(pred[48,6]{1,0:T(8,128)(4,1)} %copy-done.9) | copy-start | bytes 868
  531.2 7.8 %copy-start.4 = (bf16[2,48,6,4,256]{4,3,0,2,1:T(4,128)(2,1)S(1)}, bf16[2,48,6,4,256]{4,3,0,2,1:T(4,128)(2,1)}, u32[]{:S(2)}) copy-start(bf16[2,48,6,4,256]{4,3,0,2,1:T(4,128)(2,1)} %get-tuple-element.8) | copy-start | bytes 3538948
  531.2 7.8 %copy-start.20 = (bf16[2,6,4,256]{3,2,1,0:T(4,128)(2,1)S(1)}, bf16[2,6,4,256]{3,2,1,0:T(4,128)(2,1)}, u32[]{:S(2)}) copy-start(bf16[2,6,4,256]{3,2,1,0:T(4,128)(2,1)} %get-tuple-element.16) | copy-start | bytes 73732
  604.2 6.0 copy-start.19
  637.8 10.6 %copy-start.2 = (bf16[288,16,256]{2,1,0:T(8,128)(2,1)S(1)}, bf16[288,16,256]{2,1,0:T(8,128)(2,1)}, u32[]{:S(2)}) copy-start(bf16[288,16,256]{2,1,0:T(8,128)(2,1)} %gather_fusion.7) | copy-start | bytes 7077892
  637.8 10.6 %copy-start.11 = (pred[48,6]{1,0:T(8,128)(4,1)S(1)}, pred[48,6]{1,0:T(8,128)(4,1)}, u32[]{:S(2)}) copy-start(pred[48,6]{1,0:T(8,128)(4,1)} %copy-done.9) | copy-start | bytes 868
  637.8 10.6 %copy-start.12 = (f32[6,48,16]{2,1,0:T(8,128)S(1)}, f32[6,48,16]{2,1,0:T(8,128)}, u32[]{:S(2)}) copy-start(f32[6,48,16]{2,1,0:T(8,128)} %copy.147) | copy-start | bytes 55300
  637.8 10.6 %copy-start.29 = (pred[48,6]{0,1:T(8,128)(4,1)S(1)}, pred[48,6]{0,1:T(8,128)(4,1)}, u32[]{:S(2)}) copy-start(pred[48,6]{0,1:T(8,128)(4,1)} %get-tuple-element.27) | copy-start | bytes 868
  648.5 106.6 %copy-start.1 = (s32[3,6,48]{2,1,0:T(8,128)S(1)}, s32[3,6,48]{2,1,0:T(8,128)}, u32[]{:S(2)}) copy-start(s32[3,6,48]{2,1,0:T(8,128)} %param.10) | copy-start | bytes 10372
  654.7 55.8 %collective-permute-start.5 = (f32[16,3,48]{2,0,1:T(8,128)S(1)}, f32[16,3,48]{2,0,1:T(8,128)S(1)}, u32[]{:S(2)}, u32[]{:S(2)}) collective-permute-start(f32[16,3,48]{2,0,1:T(8,128)S(1)} %fusion.71), channel_id=1, source_target_pairs={{0,8},{1,9},{2,10},{3,11},{4,12},{5,13},{6,14},{7,15},{16,24},{17,... | collective-permute-start | bytes 27656 | tf_op jit(solution)/shard_map/ppermute | solution.py:17
  (17 other events, 69.4 us)
Sparse Core Ops, SparseCore 0:
  9.7 38.6 all-gather.7
  50.1 358.9 all-gather.5
